TPU v7x, 1024 devices: a whole 8x8x8 slice. The times are simulated.
1024 devices in a mesh: rep: 8 (over x), ctx: 32 (over z, y_hi), head: 2 (over y_lo), pool: 2 (over core).
Axes of the slice: x: 8, y: 8 (y_hi: 4, y_lo: 2; y = y_hi * 2 + y_lo), z: 8, core: 2. Of those that a mesh axis runs over, the one named last changes fastest.
Arguments:
- prefix_kv: bfloat16 [32768, 4, 2, 128], P(('rep', 'ctx', 'head', 'pool')), may hold values from -24 to 24
- queries: bfloat16 [2, 2048, 32, 128], P(None, ('rep', 'ctx', 'pool'), 'head'), may hold values from -12 to 12
- suffix_cache: bfloat16 [2048, 512, 4, 2, 128], P(('rep', 'ctx', 'pool'), None, 'head'), may hold values from -8 to 8
- suffix_lengths: int32 [2048], P(('rep', 'ctx', 'pool')), may hold values from 1 to 510, as said below
Outputs:
- attention: bfloat16 [2, 2048, 32, 128], P(None, ('rep', 'ctx', 'pool'), 'head')
Inputs may be any that keep to these rules, and one draw needn't show every extreme that they name: `suffix_lengths`: some session holds exactly 510 cached tokens, so that the last step of that session reads every slot.
All inputs are finite; a program needn't handle non-finite values.
Results may differ from a plain program's by a relative error of at most 0.0049.
Values may be sent and summed in bfloat16 or wider, within the bound.
A program may use at most 32 MiB of HBM per device.

v0:
```python
import math

import jax
import jax.numpy as jnp
from jax import lax
from jax.sharding import PartitionSpec as P


def shard_partial(query_block, context):
    head_dim = query_block.shape[-1]
    scores = jnp.einsum(
        "tbkgd,lkd->tbkgl", query_block, context[:, :, 0, :], preferred_element_type=jnp.float32
    ) * (1.0 / math.sqrt(head_dim))
    top_score = jnp.max(scores, axis=-1)
    weights = jnp.exp(scores - top_score[..., None])
    weight_sum = jnp.sum(weights, axis=-1)
    accum = jnp.einsum(
        "tbkgl,lkd->tbkgd",
        weights.astype(jnp.bfloat16),
        context[:, :, 1, :],
        preferred_element_type=jnp.float32,
    )
    partial_value = (accum / weight_sum[..., None]).astype(jnp.bfloat16)
    return (partial_value, top_score + jnp.log(weight_sum))


def suffix_terms(own_queries, suffix_cache, suffix_lengths):
    step_count = own_queries.shape[0]
    head_dim = own_queries.shape[-1]
    slot_count = suffix_cache.shape[1]
    scores = jnp.einsum(
        "tskgd,sjkd->tskgj",
        own_queries,
        suffix_cache[:, :, :, 0, :],
        preferred_element_type=jnp.float32,
    ) * (1.0 / math.sqrt(head_dim))
    positions = jnp.arange(slot_count, dtype=jnp.int32)
    last_pos = suffix_lengths[None, :] + jnp.arange(step_count, dtype=jnp.int32)[:, None]
    visible = (positions[None, None, :] <= last_pos[:, :, None])[:, :, None, None, :]
    masked = jnp.where(visible, scores, -jnp.inf)
    top_score = jnp.max(masked, axis=-1)
    weights = jnp.exp(masked - top_score[..., None])
    weight_sum = jnp.sum(weights, axis=-1)
    accum = jnp.einsum(
        "tskgj,sjkd->tskgd",
        weights.astype(jnp.bfloat16),
        suffix_cache[:, :, :, 1, :],
        preferred_element_type=jnp.float32,
    )
    return (top_score, weight_sum, accum)


def local(prefix_kv, queries, suffix_cache, suffix_lengths):
    all_heads = lax.all_gather(prefix_kv, ("rep", "pool"), axis=0, tiled=True)
    context = lax.all_to_all(all_heads, "head", split_axis=1, concat_axis=0, tiled=True)
    step_count, sess_dev, heads_dev, head_dim = queries.shape
    kv_heads = context.shape[1]
    group_size = heads_dev // kv_heads
    ctx_count = lax.axis_size("ctx")
    gathered = lax.all_gather(queries, "ctx", axis=1, tiled=True)
    sessions_all = ctx_count * sess_dev
    block_size = min(sessions_all, max(1, 512 // (step_count * heads_dev)))
    while sessions_all % block_size:
        block_size -= 1
    blocks = jnp.moveaxis(
        gathered.reshape(
            step_count, sessions_all // block_size, block_size, kv_heads, group_size, head_dim
        ),
        1,
        0,
    )
    partials, log_totals = lax.map(lambda query_block: shard_partial(query_block, context), blocks)
    partials = jnp.moveaxis(partials, 0, 1).reshape(
        step_count, ctx_count, sess_dev, kv_heads, group_size, head_dim
    )
    log_totals = jnp.moveaxis(log_totals, 0, 1).reshape(
        step_count, ctx_count, sess_dev, kv_heads, group_size
    )
    own_queries = queries.reshape(step_count, sess_dev, kv_heads, group_size, head_dim)
    suffix_top, suffix_sum, suffix_accum = suffix_terms(own_queries, suffix_cache, suffix_lengths)
    prefix_top_all = lax.pmax(log_totals, "ctx")
    weights = jnp.exp(log_totals - prefix_top_all)
    summed, denoms = (
        lax.psum_scatter(
            weights[..., None] * partials.astype(jnp.float32),
            "ctx",
            scatter_dimension=1,
            tiled=True,
        ),
        lax.psum_scatter(weights, "ctx", scatter_dimension=1, tiled=True),
    )
    weighted = summed[:, 0]
    weight_total = denoms[:, 0]
    prefix_top = lax.dynamic_index_in_dim(prefix_top_all, lax.axis_index("ctx"), 1, keepdims=False)
    top_all = jnp.maximum(prefix_top, suffix_top)
    prefix_factor = jnp.exp(prefix_top - top_all)
    suffix_factor = jnp.exp(suffix_top - top_all)
    numerator = weighted * prefix_factor[..., None] + suffix_factor[..., None] * suffix_accum
    denominator = weight_total * prefix_factor + suffix_factor * suffix_sum
    result = (numerator / denominator[..., None]).astype(jnp.bfloat16)
    return result.reshape(step_count, sess_dev, heads_dev, head_dim)


def solution(mesh):
    return jax.shard_map(
        local,
        mesh=mesh,
        in_specs=(
            P(("rep", "ctx", "head", "pool"), None, None, None),
            P(None, ("rep", "ctx", "pool"), "head", None),
            P(("rep", "ctx", "pool"), None, "head", None, None),
            P(("rep", "ctx", "pool")),
        ),
        out_specs=P(None, ("rep", "ctx", "pool"), "head", None),
        check_vma=False,
    )
```

profile of v0, /device:TPU:1, one launch (start us, length us, event | category | flops | bytes accessed | tf_op | source)
XLA Modules:
  0.0 573.2 jit_solution(13162452608553889943)
XLA Ops:
  6.5 1.5 copy.46
  8.1 0.7 all-gather.3.cloned.1.call-update
  8.8 57.2 %all-gather.5.cloned.1.call-done = bf16[512,4,2,128]{3,1,2,0:T(4,128)(2,1)} async-done(((bf16[32,4,2,128]{3,1,2,0:T(4,128)(2,1)}), bf16[512,4,2,128]{3,1,2,0:T(4,128)(2,1)}) %all-gather.5.cloned.1.call-update) | async-done | bytes 1048592 | tf_op jit(solution)/shard_map/all_gather | solution.py:54
  66.0 3.0 copy.47
  69.0 3.6 all-to-all-start
  72.7 13.4 %all-to-all-done = bf16[512,4,2,128]{3,2,0,1:T(2,128)(2,1)S(1)} async-done(((bf16[512,4,2,128]{3,2,0,1:T(2,128)(2,1)}), bf16[512,4,2,128]{3,2,0,1:T(2,128)(2,1)S(1)}, u32[]{:S(2)}, u32[]{:S(2)}) %all-to-all-start) | async-done | bytes 1048608 | tf_op jit(solution)/shard_map/all_to_all | solution.py:55
  86.1 0.1 copy.48
  86.2 69.8 %all-gather.3.cloned.1.call-done = bf16[2,128,16,128]{3,2,1,0:T(8,128)(2,1)} async-done(((bf16[2,4,16,128]{3,2,1,0:T(8,128)(2,1)}), bf16[2,128,16,128]{3,2,1,0:T(8,128)(2,1)}) %all-gather.3.cloned.1.call-update) | async-done | bytes 1048592 | tf_op jit(solution)/shard_map/all_gather | solution.py:60
  156.0 20.6 %while.12 = (s32[]{:T(128)}, bf16[8,2,16,2,8,128]{5,4,2,1,3,0:T(8,128)(2,1)S(1)}, f32[8,2,16,2,8]{4,2,1,3,0:T(8,128)S(1)}, bf16[8,2,16,2,8,128]{5,4,3,2,0,1:T(8,...) while((s32[]{:T(128)}, bf16[8,2,16,2,8,128]{5,4,2,1,3,0:T(8,128)(2,1)S(1)}, ...), condition=%wide.region_3.4_spmd, body=%wide.region_0.3_spmd.sunk | while | flops 272760320 | bytes 7772249 | solution.py:72
  156.0 1.4 bitcast_reduce_fusion.2
  157.4 0.5 fusion.42
  157.9 0.6 fusion.43
  158.5 1.4 bitcast_reduce_fusion.2
  160.0 0.5 fusion.42
  160.5 0.6 fusion.43
  161.1 1.4 bitcast_reduce_fusion.2
  162.5 0.5 fusion.42
  163.1 0.6 fusion.43
  163.7 1.4 bitcast_reduce_fusion.2
  165.1 0.5 fusion.42
  165.6 0.6 fusion.43
  166.3 1.4 bitcast_reduce_fusion.2
  167.7 0.5 fusion.42
  168.2 0.6 fusion.43
  168.8 1.4 bitcast_reduce_fusion.2
  170.3 0.5 fusion.42
  170.8 0.6 fusion.43
  171.4 1.4 bitcast_reduce_fusion.2
  172.9 0.5 fusion.42
  173.4 0.6 fusion.43
  174.0 1.4 bitcast_reduce_fusion.2
  175.4 0.5 fusion.42
  175.9 0.6 fusion.43
  176.6 0.9 copy-done.2
  177.6 129.8 %pmax.7 = f32[2,32,4,2,8]{4,2,1,3,0:T(4,128)S(1)} all-reduce(f32[2,32,4,2,8]{4,2,1,3,0:T(4,128)S(1)} %bitcast.138), channel_id=1, replica_groups=mesh['rep'=8,'ctx'=32,'head'=2,'pool'=2] {'ctx'}, use_global_device_ids=true, to_apply=%region_4.5 | all-reduce | flops 4096 | bytes 32768 | tf_op jit(solution)/shard_map/pmax | solution.py:81
  307.4 0.2 copy.51
  307.6 0.2 convert_bitcast_fusion
  307.9 0.3 copy.52
  308.1 2.0 broadcast_multiply_fusion
  310.1 1.4 dynamic-slice
  311.7 3.8 fusion.33
  315.6 0.5 fusion.34
  316.0 0.2 fusion.22
  316.3 126.0 %all-reduce = f32[2,32,4,2,8]{4,2,1,3,0:T(4,128)S(1)} all-reduce(f32[2,32,4,2,8]{4,2,1,3,0:T(4,128)S(1)} %bitcast.137), channel_id=3, replica_groups=mesh['rep'=8,'ctx'=32,'head'=2,'pool'=2] {'ctx'}, use_global_device_ids=true, to_apply=%region_7.8.clone | all-reduce | flops 4096 | bytes 32768
  442.3 0.7 fusion.30
  443.0 121.9 %reduce-scatter.3.cloned.1.call-done = f32[2,1,4,2,8,128]{5,4,0,3,2,1:T(8,128)} async-done(((f32[2,32,4,2,8,128]{5,4,0,3,2,1:T(8,128)}), f32[2,1,4,2,8,128]{5,4,0,3,2,1:T(8,128)}) %reduce-scatter.3.cloned.1.call-update) | async-done | bytes 65552 | tf_op jit(solution)/shard_map/reduce_scatter | solution.py:84
  564.9 1.2 fusion.21
  566.1 0.6 copy.105
  (35 shorter events, 0.5 us)
Async XLA Ops:
  6.5 59.5 %all-gather.5.cloned.1.call-start = ((), (), s32[]{:S(2)}) async-start(), calls=%async_computation.3 | async-start | bytes 1114112 | tf_op jit(solution)/shard_map/all_gather | solution.py:54
  8.0 147.9 %all-gather.3.cloned.1.call-start = ((), (), s32[]{:S(2)}) async-start(), calls=%async_computation.2 | async-start | bytes 1081344 | tf_op jit(solution)/shard_map/all_gather | solution.py:60
  69.0 17.0 %all-to-all-start = ((bf16[512,4,2,128]{3,2,0,1:T(2,128)(2,1)}), bf16[512,4,2,128]{3,2,0,1:T(2,128)(2,1)S(1)}, u32[]{:S(2)}, u32[]{:S(2)}) async-start(bf16[512,4,2,128]{3,2,0,1:T(2,128)(2,1)} %copy.47), calls=%async_computation | async-start | bytes 2097152 | tf_op jit(solution)/shard_map/all_to_all | solution.py:55
  72.6 492.3 %reduce-scatter.3.cloned.1.call-start = ((), (), s32[]{:S(2)}) async-start(), calls=%async_computation.4 | async-start | bytes 2162688 | tf_op jit(solution)/shard_map/reduce_scatter | solution.py:84
  176.6 1.0 copy-start.2
  177.5 130.1 %copy-start.3 = (bf16[8,2,16,2,8,128]{5,4,2,1,3,0:T(8,128)(2,1)S(1)}, bf16[8,2,16,2,8,128]{5,4,2,1,3,0:T(8,128)(2,1)}, u32[]{:S(2)}) copy-start(bf16[8,2,16,2,8,128]{5,4,2,1,3,0:T(8,128)(2,1)} %copy-done.2) | copy-start | bytes 3145732
  310.1 1.5 copy-start.5
  310.1 1.6 copy-start
  311.7 3.8 copy-start.4
  315.5 249.4 %copy-start.1 = (bf16[4,512,2,1,128]{4,3,2,1,0:T(2,128)(2,1)S(1)}, bf16[4,512,2,1,128]{4,3,2,1,0:T(2,128)(2,1)}, u32[]{:S(2)}) copy-start(bf16[4,512,2,1,128]{4,3,2,1,0:T(2,128)(2,1)} %get-tuple-element.66) | copy-start | bytes 3145732
Sparse Core Ops, SparseCore 0:
  10.1 55.8 all-gather.4
  70.3 85.6 all-gather.2
  310.2 254.6 reduce-scatter.2
where the time goes:
time: 578 us; the launch traced here: 573 us
  waiting for transfers between devices  263 us (46%)
  blocking collectives  256 us (44%)
  matrix products  17.8 us (3%)
  between operations  13.3 us (2%)
  local copies, waits for them, and re-layouts  12 us (2%)
  other arithmetic  7.41 us (1%)
    pmax x1, blocking collectives, local(): prefix_top_all = lax.pmax(log_totals, 'ctx')  130 us
    unnamed x1, blocking collectives  126 us
    reduce_scatter x1, waiting for transfers between devices, local(): lax.psum_scatter(weights[..., None] * partials.astype(jnp.float32), 'ctx'...  122 us
    all_gather x1, waiting for transfers between devices, local(): gathered = lax.all_gather(queries, 'ctx', axis=1, tiled=True)  69.8 us
    all_gather x1, waiting for transfers between devices, local(): all_heads = lax.all_gather(prefix_kv, ('rep', 'pool'), axis=0, tiled=True)  57.2 us
    all_to_all x1, waiting for transfers between devices, local(): lax.all_to_all(all_heads, 'head', split_axis=1, concat_axis=0, tiled=True)  13.4 us
  transfers between devices with their start and end apart: 4, of which 4 were waited for; matrix products, arithmetic and copies ran while one was open for 2% of the time, Pallas kernels for 0%

commit v1 on v0

v1 whole, which is shorter than its diff:
```python
import functools
import math

import jax
import jax.numpy as jnp
from jax import lax
from jax.experimental import pallas as pl
from jax.experimental.pallas import tpu as pltpu
from jax.sharding import PartitionSpec as P

MESH = pl.DeviceIdType.MESH
F32 = jnp.float32
BF16 = jnp.bfloat16
HD = 128
RING = 8
SCALE = 1.0 / math.sqrt(HD)
LOG2E = 1.0 / math.log(2.0)
ORDER = (0, 1, 7, 2, 6, 3, 5, 4)


def wrap(v):
    return lax.rem(v + 2 * RING, RING)


def kernel(
    pre_ref, q_ref, len_ref, suf_hbm, out_ref,
    kvbuf, kvf, kvsrc, qsrc, qbuf, sufbuf, top, tot, acc, osrc, lsrc, obuf, lbuf,
    sacc, smax, ssum, ob,
    suf_sem, send_sem, y_sem, q_sem, xr_sem, xl_sem, o_sem, l_sem,
):
    x = lax.axis_index("rep")
    c = lax.axis_index("ctx")
    hd = lax.axis_index("head")
    core = lax.axis_index("pool")
    z = lax.div(c, 4)
    y = lax.rem(c, 4) * 2 + hd

    def device(xx, yy, zz, cc):
        return (xx, zz * 4 + lax.div(yy, 2), lax.rem(yy, 2), cc)

    ypeers = [(i, d, cc) for i, d in enumerate(ORDER) for cc in (0, 1) if (d, cc) != (0, 0)]
    zpeers = [(d, cc) for d in ORDER for cc in (0, 1) if (d, cc) != (0, 0)]

    def other(cc):
        return lax.rem(core + cc, 2)

    barrier = pltpu.get_barrier_semaphore()
    greet = [device(x, wrap(y + d), z, other(cc)) for _, d, cc in ypeers]
    greet += [device(x, y, wrap(z + d), other(cc)) for d, cc in zpeers if d]
    greet += [device(wrap(x + 1), y, z, core), device(wrap(x - 1), y, z, core)]
    for dev in greet:
        pl.semaphore_signal(barrier, inc=1, device_id=dev, device_id_type=MESH)

    suffix_copy = pltpu.make_async_copy(suf_hbm, sufbuf, suf_sem)
    suffix_copy.start()

    kvf[...] = pre_ref[...].astype(F32)
    for r in range(8):
        kvsrc[r // 2, r % 2] = kvf[pl.ds(r, 32, stride=8), :].astype(BF16)
    my_head = 2 * hd + core
    kvbuf[x, 0] = kvsrc[my_head]
    q8 = q_ref[...].reshape(8, 16, HD).astype(F32)
    for k in range(2):
        qsrc[k] = q8[:, 8 * k : 8 * k + 8, :].reshape(64, HD).astype(BF16)
    qbuf[0] = qsrc[core]
    top[...] = jnp.full_like(top, -jnp.inf)
    tot[...] = jnp.zeros_like(tot)
    acc[...] = jnp.zeros_like(acc)

    pl.semaphore_wait(barrier, len(greet))

    sends = []

    def remote(src, dst, recv, dev):
        copy = pltpu.make_async_remote_copy(
            src_ref=src, dst_ref=dst, send_sem=send_sem.at[len(sends)], recv_sem=recv,
            device_id=dev, device_id_type=MESH,
        )
        copy.start()
        sends.append(copy)

    slot_of = {d: i for i, d in enumerate(ORDER)}
    for i, d, cc in ypeers:
        yy, pc = wrap(y + d), other(cc)
        slot = slot_of[(-d) % RING] * 2 + cc
        remote(
            kvsrc.at[2 * lax.rem(yy, 2) + pc], kvbuf.at[x, slot],
            y_sem.at[slot // 4], device(x, yy, z, pc),
        )
    for d, cc in zpeers:
        pc = other(cc)
        slot = ((-d) % RING) * 2 + cc
        remote(qsrc.at[pc], qbuf.at[slot], q_sem, device(x, y, wrap(z + d), pc))

    suffix_copy.wait()
    row = lax.broadcasted_iota(jnp.int32, (32, 2048), 0)
    col = lax.broadcasted_iota(jnp.int32, (32, 2048), 1)
    base_ok = jnp.logical_and((col & 1) == 0, ((col >> 1) & 1) == ((row >> 3) & 1))
    reach = (col >> 2) - (row >> 4)
    for n in range(4):
        kv = sufbuf[n]
        qn = q_ref[:, n].reshape(32, HD)
        s = lax.dot_general(qn, kv, (((1,), (1,)), ((), ())), preferred_element_type=F32)
        ok = jnp.logical_and(base_ok, reach <= len_ref[n])
        s = jnp.where(ok, s, -jnp.inf)
        mx = jnp.max(s, axis=1, keepdims=True)
        p = jnp.exp2((s - mx) * (SCALE * LOG2E))
        sm = jnp.sum(p, axis=1, keepdims=True)
        pb = pltpu.roll(p, 1, 1).astype(BF16)
        a = jnp.dot(pb, kv, preferred_element_type=F32)
        mxb = jnp.broadcast_to(mx * SCALE, (32, HD))
        smb = jnp.broadcast_to(sm, (32, HD))
        for t in range(2):
            for k in range(2):
                lo = 16 * t + 8 * k
                sacc[k, 4 * t + n] = a[lo : lo + 8]
                smax[k, 4 * t + n] = mxb[lo : lo + 8]
                ssum[k, 4 * t + n] = smb[lo : lo + 8]

    right, left = device(wrap(x + 1), y, z, core), device(wrap(x - 1), y, z, core)

    def hop(i, slot, g, to_right):
        sem = xr_sem if to_right else xl_sem
        ref = kvbuf.at[slot, pl.ds(4 * g, 4)]
        return pltpu.make_async_remote_copy(
            src_ref=ref, dst_ref=ref, send_sem=sem.at[0, i], recv_sem=sem.at[1, i],
            device_id=right if to_right else left, device_id_type=MESH,
        )

    def unit(sa, ga, sb, gb):
        def part(slot, g, which):
            return kvbuf[slot, pl.ds(4 * g, 4), which].reshape(128, HD)

        k = jnp.concatenate([part(sa, ga, 0), part(sb, gb, 0)], axis=0)
        v = jnp.concatenate([part(sa, ga, 1), part(sb, gb, 1)], axis=0)

        def rows(i, carry):
            r = pl.ds(pl.multiple_of(i * 256, 256), 256)
            q = qbuf[pl.ds(4 * i, 4)].reshape(256, HD)
            s = lax.dot_general(q, k, (((1,), (1,)), ((), ())), preferred_element_type=F32)
            old = top[r, :]
            new = jnp.maximum(old, jnp.max(s, axis=1, keepdims=True))
            p = jnp.exp2((s - jnp.concatenate([new, new], axis=1)) * (SCALE * LOG2E))
            keep = jnp.exp2((old - new) * (SCALE * LOG2E))
            top[r, :] = new
            tot[r, :] = tot[r, :] * keep + (p[:, :128] + p[:, 128:])
            acc[r, :] = acc[r, :] * keep + jnp.dot(p.astype(BF16), v, preferred_element_type=F32)
            return carry

        lax.fori_loop(0, 4, rows, 0)

    for g in range(4):
        lo = 1 if g == 0 else 4 * g
        piece = kvbuf.at[x, pl.ds(lo, 4 * g + 4 - lo)]
        pltpu.make_async_copy(piece, piece, y_sem.at[g]).wait()
        hop(g, x, g, True).start()
        hop(g, x, g, False).start()
    pltpu.make_async_copy(qbuf.at[pl.ds(1, 15)], qbuf.at[pl.ds(1, 15)], q_sem).wait()
    unit(x, 0, x, 1)
    unit(x, 2, x, 3)

    def middle(i, carry):
        h = lax.div(i, 4) + 1
        g = lax.rem(i, 4)
        sl, sr = wrap(x - h), wrap(x + h)
        hop(i, sl, g, True).wait_recv()

        @pl.when(jnp.logical_or(h < 3, g < 2))
        def _():
            hop(i + 4, sl, g, True).start()

        hop(i, sr, g, False).wait_recv()

        @pl.when(h < 3)
        def _():
            hop(i + 4, sr, g, False).start()

        @pl.when(jnp.logical_and(h == 3, g >= 2))
        def _():
            hop(i + 2, sr, g, False).start()

        unit(sl, g, sr, g)
        return carry

    lax.fori_loop(0, 12, middle, 0)
    far = wrap(x + 4)
    for g in range(2):
        hop(12 + g, far, g, True).wait_recv()
        hop(12 + g, far, g + 2, False).wait_recv()
        unit(far, g, far, g + 2)

    eye = lax.broadcasted_iota(jnp.int32, (64, HD), 0) == lax.broadcasted_iota(
        jnp.int32, (64, HD), 1
    )

    def finish(s):
        r = pl.ds(64 * s, 64)
        whole = jnp.sum(tot[r, :], axis=1, keepdims=True)
        osrc[s] = (acc[r, :] / whole).astype(BF16)
        lse = top[r, :] * SCALE + jnp.log(whole)
        lsrc[s] = jnp.sum(jnp.where(eye, lse, 0.0), axis=0, keepdims=True)

    def give(d, cc):
        pc, s = other(cc), 2 * d + cc
        dev = device(x, y, wrap(z + d), pc)
        slot = ((-d) % RING) * 2 + cc
        remote(lsrc.at[s], lbuf.at[slot], l_sem, dev)
        remote(osrc.at[s], obuf.at[slot], o_sem, dev)

    order = list(reversed(zpeers))
    finish(2 * order[0][0] + order[0][1])
    for here, after in zip(order, order[1:] + [(0, 0)]):
        finish(2 * after[0] + after[1])
        give(*here)
    obuf[0] = osrc[0]
    lbuf[0] = lsrc[0]

    pltpu.make_async_copy(lbuf.at[pl.ds(1, 15)], lbuf.at[pl.ds(1, 15)], l_sem).wait()
    pltpu.make_async_copy(obuf.at[pl.ds(1, 15)], obuf.at[pl.ds(1, 15)], o_sem).wait()
    for kk in range(2):
        k = other(kk)
        sx = smax[k].reshape(64, HD)
        lses = []
        for d in range(RING):
            spread = jnp.where(eye, lbuf[2 * d + kk], 0.0)
            lses.append(jnp.sum(spread, axis=1, keepdims=True))
        best = sx
        for v in lses:
            best = jnp.maximum(best, v)
        w = jnp.exp2((sx - best) * LOG2E)
        num = w * sacc[k].reshape(64, HD)
        den = w * ssum[k].reshape(64, HD)
        for d in range(RING):
            w = jnp.exp2((lses[d] - best) * LOG2E)
            num = num + w * obuf[2 * d + kk].astype(F32)
            den = den + w
        ob[k] = (num / den).reshape(8, 8, HD)
    both = jnp.stack([ob[0], ob[1]], axis=1).reshape(8, 16, HD)
    out_ref[...] = both.astype(BF16).reshape(2, 4, 16, HD)

    for copy in sends:
        copy.wait_send()

    def drain(i, carry):
        hop(i, x, 0, True).wait_send()
        hop(i, x, 0, False).wait_send()
        return carry

    lax.fori_loop(0, 14, drain, 0)


def local(prefix_kv, queries, suffix_cache, suffix_lengths):
    vmem = pl.BlockSpec(memory_space=pltpu.VMEM)
    dma = pltpu.SemaphoreType.DMA
    return pl.pallas_call(
        kernel,
        out_shape=jax.ShapeDtypeStruct(queries.shape, BF16),
        in_specs=[
            vmem, vmem, pl.BlockSpec(memory_space=pltpu.SMEM), pl.BlockSpec(memory_space=pl.ANY),
        ],
        out_specs=vmem,
        scratch_shapes=[
            pltpu.VMEM((8, 16, 2, 32, HD), BF16),
            pltpu.VMEM((256, HD), F32),
            pltpu.VMEM((4, 2, 32, HD), BF16),
            pltpu.VMEM((2, 64, HD), BF16),
            pltpu.VMEM((16, 64, HD), BF16),
            pltpu.VMEM((4, 2048, HD), BF16),
            pltpu.VMEM((1024, HD), F32),
            pltpu.VMEM((1024, HD), F32),
            pltpu.VMEM((1024, HD), F32),
            pltpu.VMEM((16, 64, HD), BF16),
            pltpu.VMEM((16, 1, HD), F32),
            pltpu.VMEM((16, 64, HD), BF16),
            pltpu.VMEM((16, 1, HD), F32),
            pltpu.VMEM((2, 8, 8, HD), F32),
            pltpu.VMEM((2, 8, 8, HD), F32),
            pltpu.VMEM((2, 8, 8, HD), F32),
            pltpu.VMEM((2, 8, 8, HD), F32),
            dma, dma((60,)), dma((4,)), dma, dma((2, 14)), dma((2, 14)), dma, dma,
        ],
        compiler_params=pltpu.CompilerParams(
            collective_id=0, has_side_effects=True, vmem_limit_bytes=48 * 1024 * 1024
        ),
    )(
        prefix_kv.reshape(256, HD), queries, suffix_lengths,
        suffix_cache.reshape(4, 2048, HD),
    )


def solution(mesh):
    return jax.shard_map(
        local,
        mesh=mesh,
        in_specs=(
            P(("rep", "ctx", "head", "pool"), None, None, None),
            P(None, ("rep", "ctx", "pool"), "head", None),
            P(("rep", "ctx", "pool"), None, "head", None, None),
            P(("rep", "ctx", "pool")),
        ),
        out_specs=P(None, ("rep", "ctx", "pool"), "head", None),
        check_vma=False,
    )
```

time: 578 us -> 73.5 us (0.13)
  waiting for transfers between devices: 263 us -> 0 us
  blocking collectives: 256 us -> 0 us
  Pallas kernels: 0 us -> 68.3 us
  matrix products: 17.8 us -> 0 us
  between operations: 13.3 us -> 0.01 us
  local copies, waits for them, and re-layouts: 12 us -> 4.46 us
  other arithmetic: 7.41 us -> 0 us
    pmax x1 -> x0, blocking collectives: 130 us -> none  [local(): prefix_top_all = lax.pmax(log_totals, 'ctx')]
    all_gather x2 -> x0, waiting for transfers between devices: 127 us -> none  [the longest x1 69.8 us: local(): gathered = lax.all_gather(queries, 'ctx', axis=1, tiled=True)]
    unnamed x1 -> x0, blocking collectives: 126 us -> none
    reduce_scatter x1 -> x0, waiting for transfers between devices: 122 us -> none  [local(): lax.psum_scatter(weights[..., None] * partials.astype(jnp.float32), 'ctx'...]
    pallas_call x0 -> x1, Pallas kernels: none -> 68.3 us  [local(): pl.pallas_call(kernel, out_shape=jax.ShapeDtypeStruct(queries.shape, BF16...]
    dot_general x18 -> x0, matrix products: 17.8 us -> none  [the longest x8 11.4 us: shard_partial(): jnp.einsum('tbkgd,lkd->tbkgl', query_block, context[:, :, 0, :], preferre...]
    all_to_all x1 -> x0, waiting for transfers between devices: 13.4 us -> none  [local(): lax.all_to_all(all_heads, 'head', split_axis=1, concat_axis=0, tiled=True)]
  transfers between devices with their start and end apart: 4 -> 0, of which waited for: 4 -> 0; matrix products, arithmetic and copies ran while one was open for 2% -> 0% of each run, Pallas kernels for 0% -> 0%
where the time goes in v1:
time: 73.5 us; the launch traced here: 72.8 us
  Pallas kernels  68.3 us (93%)
  local copies, waits for them, and re-layouts  4.46 us (6%)
    pallas_call x1, Pallas kernels, local(): pl.pallas_call(kernel, out_shape=jax.ShapeDtypeStruct(queries.shape, BF16...  68.3 us
    unnamed x9, local copies, waits for them, and re-layouts  4.46 us

profile of v1, /device:TPU:1, one launch (start us, length us, event | category | flops | bytes accessed | tf_op | source)
XLA Modules:
  0.0 72.8 jit_solution(13004821910697323852)
XLA Ops:
  0.0 0.0 copy-start
  0.0 1.6 %copy-done = bf16[4,512,2,2,128]{4,3,2,1,0:T(2,128)(2,1)S(1)} copy-done((bf16[4,512,2,2,128]{4,3,2,1,0:T(2,128)(2,1)S(1)}, bf16[4,512,2,2,128]{4,3,2,1,0:T(2,128)(2,1)}, u32[]{:S(2)}) %copy-start) | copy-done | bytes 2097176
  1.6 0.0 copy-start.1
  1.6 0.8 %copy-done.1 = bf16[32,4,2,128]{3,2,1,0:T(2,128)(2,1)S(1)} copy-done((bf16[32,4,2,128]{3,2,1,0:T(2,128)(2,1)S(1)}, bf16[32,4,2,128]{3,2,1,0:T(2,128)(2,1)}, u32[]{:S(2)}) %copy-start.1) | copy-done | bytes 65560
  2.4 0.0 copy-start.2
  2.4 0.8 %copy-done.2 = bf16[2,4,16,128]{3,2,1,0:T(8,128)(2,1)S(1)} copy-done((bf16[2,4,16,128]{3,2,1,0:T(8,128)(2,1)S(1)}, bf16[2,4,16,128]{3,2,1,0:T(8,128)(2,1)}, u32[]{:S(2)}) %copy-start.2) | copy-done | bytes 32792
  3.2 0.0 copy-start.3
  3.2 0.7 copy-done.3
  3.8 68.3 %shard_map.46 = bf16[2,4,16,128]{3,2,1,0:T(8,128)(2,1)S(1)} custom-call(bf16[256,128]{1,0:T(8,128)(2,1)S(1)} %bitcast.3, bf16[2,4,16,128]{3,2,1,0:T(8,128)(2,1)S(1)} %copy-done.2, s32[4]{0:T(128)S(1)} %copy-done.3, bf16[4,2048,128]{2,1,0:T(8,128)(2,1)S(1)} %bitcast.2), custom_call_target="tpu_custom_call" | custom-call | tf_op jit(solution)/shard_map/pallas_call | solution.py:255
  72.2 0.6 copy.6
Async XLA Ops:
  0.0 1.6 %copy-start = (bf16[4,512,2,2,128]{4,3,2,1,0:T(2,128)(2,1)S(1)}, bf16[4,512,2,2,128]{4,3,2,1,0:T(2,128)(2,1)}, u32[]{:S(2)}) copy-start(bf16[4,512,2,2,128]{4,3,2,1,0:T(2,128)(2,1)} %param.6) | copy-start | bytes 6291460
  1.6 0.8 %copy-start.1 = (bf16[32,4,2,128]{3,2,1,0:T(2,128)(2,1)S(1)}, bf16[32,4,2,128]{3,2,1,0:T(2,128)(2,1)}, u32[]{:S(2)}) copy-start(bf16[32,4,2,128]{3,2,1,0:T(2,128)(2,1)} %param.4) | copy-start | bytes 196612
  2.4 0.8 %copy-start.2 = (bf16[2,4,16,128]{3,2,1,0:T(8,128)(2,1)S(1)}, bf16[2,4,16,128]{3,2,1,0:T(8,128)(2,1)}, u32[]{:S(2)}) copy-start(bf16[2,4,16,128]{3,2,1,0:T(8,128)(2,1)} %q_ref.1) | copy-start | bytes 98308
  3.2 0.7 copy-start.3

commit v2 on v1

--- a/solution.py
+++ b/solution.py
@@ -23,10 +23,10 @@
 
 
 def kernel(
-    pre_ref, q_ref, len_ref, suf_hbm, out_ref,
-    kvbuf, kvf, kvsrc, qsrc, qbuf, sufbuf, top, tot, acc, osrc, lsrc, obuf, lbuf,
+    pre_hbm, q_hbm, len_hbm, suf_hbm, out_ref,
+    pre_ref, q_ref, len_ref, kvbuf, kvf, kvsrc, qsrc, qbuf, sufbuf, top, tot, acc, osrc, lsrc, obuf, lbuf,
     sacc, smax, ssum, ob,
-    suf_sem, send_sem, y_sem, q_sem, xr_sem, xl_sem, o_sem, l_sem,
+    in_sem, send_sem, y_sem, q_sem, xr_sem, xl_sem, o_sem, l_sem,
 ):
     x = lax.axis_index("rep")
     c = lax.axis_index("ctx")
@@ -44,6 +44,15 @@
     def other(cc):
         return lax.rem(core + cc, 2)
 
+    fetch = [
+        pltpu.make_async_copy(src, dst, in_sem.at[i])
+        for i, (src, dst) in enumerate(
+            [(pre_hbm, pre_ref), (q_hbm, q_ref), (len_hbm, len_ref), (suf_hbm, sufbuf)]
+        )
+    ]
+    for copy in fetch:
+        copy.start()
+
     barrier = pltpu.get_barrier_semaphore()
     greet = [device(x, wrap(y + d), z, other(cc)) for _, d, cc in ypeers]
     greet += [device(x, y, wrap(z + d), other(cc)) for d, cc in zpeers if d]
@@ -51,9 +60,8 @@
     for dev in greet:
         pl.semaphore_signal(barrier, inc=1, device_id=dev, device_id_type=MESH)
 
-    suffix_copy = pltpu.make_async_copy(suf_hbm, sufbuf, suf_sem)
-    suffix_copy.start()
-
+    fetch[0].wait()
+    fetch[1].wait()
     kvf[...] = pre_ref[...].astype(F32)
     for r in range(8):
         kvsrc[r // 2, r % 2] = kvf[pl.ds(r, 32, stride=8), :].astype(BF16)
@@ -62,10 +70,7 @@
     q8 = q_ref[...].reshape(8, 16, HD).astype(F32)
     for k in range(2):
         qsrc[k] = q8[:, 8 * k : 8 * k + 8, :].reshape(64, HD).astype(BF16)
-    qbuf[0] = qsrc[core]
-    top[...] = jnp.full_like(top, -jnp.inf)
-    tot[...] = jnp.zeros_like(tot)
-    acc[...] = jnp.zeros_like(acc)
+    qbuf[2 * z] = qsrc[core]
 
     pl.semaphore_wait(barrier, len(greet))
 
@@ -89,15 +94,24 @@
         )
     for d, cc in zpeers:
         pc = other(cc)
-        slot = ((-d) % RING) * 2 + cc
-        remote(qsrc.at[pc], qbuf.at[slot], q_sem, device(x, y, wrap(z + d), pc))
-
-    suffix_copy.wait()
+        remote(qsrc.at[pc], qbuf.at[2 * z + cc], q_sem, device(x, y, wrap(z + d), pc))
+
+    right, left = device(wrap(x + 1), y, z, core), device(wrap(x - 1), y, z, core)
+
+    def hop(i, slot, g, to_right):
+        sem = xr_sem if to_right else xl_sem
+        ref = kvbuf.at[slot, pl.ds(4 * g, 4)]
+        return pltpu.make_async_remote_copy(
+            src_ref=ref, dst_ref=ref, send_sem=sem.at[0, i], recv_sem=sem.at[1, i],
+            device_id=right if to_right else left, device_id_type=MESH,
+        )
+
     row = lax.broadcasted_iota(jnp.int32, (32, 2048), 0)
     col = lax.broadcasted_iota(jnp.int32, (32, 2048), 1)
     base_ok = jnp.logical_and((col & 1) == 0, ((col >> 1) & 1) == ((row >> 3) & 1))
     reach = (col >> 2) - (row >> 4)
-    for n in range(4):
+
+    def suffix(n):
         kv = sufbuf[n]
         qn = q_ref[:, n].reshape(32, HD)
         s = lax.dot_general(qn, kv, (((1,), (1,)), ((), ())), preferred_element_type=F32)
@@ -117,37 +131,49 @@
                 smax[k, 4 * t + n] = mxb[lo : lo + 8]
                 ssum[k, 4 * t + n] = smb[lo : lo + 8]
 
-    right, left = device(wrap(x + 1), y, z, core), device(wrap(x - 1), y, z, core)
-
-    def hop(i, slot, g, to_right):
-        sem = xr_sem if to_right else xl_sem
-        ref = kvbuf.at[slot, pl.ds(4 * g, 4)]
-        return pltpu.make_async_remote_copy(
-            src_ref=ref, dst_ref=ref, send_sem=sem.at[0, i], recv_sem=sem.at[1, i],
-            device_id=right if to_right else left, device_id_type=MESH,
-        )
-
-    def unit(sa, ga, sb, gb):
+    def unit(sa, ga, sb, gb, first=False, after=None):
         def part(slot, g, which):
             return kvbuf[slot, pl.ds(4 * g, 4), which].reshape(128, HD)
 
         k = jnp.concatenate([part(sa, ga, 0), part(sb, gb, 0)], axis=0)
-        v = jnp.concatenate([part(sa, ga, 1), part(sb, gb, 1)], axis=0)
-
-        def rows(i, carry):
-            r = pl.ds(pl.multiple_of(i * 256, 256), 256)
-            q = qbuf[pl.ds(4 * i, 4)].reshape(256, HD)
-            s = lax.dot_general(q, k, (((1,), (1,)), ((), ())), preferred_element_type=F32)
-            old = top[r, :]
-            new = jnp.maximum(old, jnp.max(s, axis=1, keepdims=True))
-            p = jnp.exp2((s - jnp.concatenate([new, new], axis=1)) * (SCALE * LOG2E))
-            keep = jnp.exp2((old - new) * (SCALE * LOG2E))
-            top[r, :] = new
-            tot[r, :] = tot[r, :] * keep + (p[:, :128] + p[:, 128:])
-            acc[r, :] = acc[r, :] * keep + jnp.dot(p.astype(BF16), v, preferred_element_type=F32)
-            return carry
-
-        lax.fori_loop(0, 4, rows, 0)
+        v = jnp.concatenate([part(sa, ga, 1), part(sb, gb, 1)], axis=0).T
+        def scores(j):
+            q = qbuf[4 * j : 4 * j + 4].reshape(256, HD)
+            return lax.dot_general(k, q, (((1,), (1,)), ((), ())), preferred_element_type=F32)
+
+        def weigh(j, s):
+            r = pl.ds(256 * j, 256)
+            new = jnp.max(s, axis=0, keepdims=True)
+            keep = None
+            if not first:
+                old = top[:, r]
+                new = jnp.maximum(old, new)
+                keep = jnp.exp2((old - new) * (SCALE * LOG2E))
+            p = jnp.exp2((s - new) * (SCALE * LOG2E))
+            part_sum = jnp.sum(p.reshape(32, 8, 256), axis=0)
+            if not first:
+                part_sum = tot[:, r] * keep + part_sum
+            top[:, r] = new
+            tot[:, r] = part_sum
+            return p.astype(BF16), keep
+
+        def gather(j, p, keep):
+            r = pl.ds(256 * j, 256)
+            o = jnp.dot(v, p, preferred_element_type=F32)
+            acc[:, r] = o if first else acc[:, r] * keep + o
+            if after:
+                after(j)
+
+        js = (0, 1, 2, 3)
+        s = scores(js[0])
+        late = None
+        for i, j in enumerate(js):
+            s_next = scores(js[i + 1]) if i < 3 else None
+            if late:
+                gather(*late)
+            late = (j, *weigh(j, s))
+            s = s_next
+        gather(*late)
 
     for g in range(4):
         lo = 1 if g == 0 else 4 * g
@@ -155,8 +181,14 @@
         pltpu.make_async_copy(piece, piece, y_sem.at[g]).wait()
         hop(g, x, g, True).start()
         hop(g, x, g, False).start()
+        if g == 0:
+            fetch[2].wait()
+            fetch[3].wait()
+        if g < 2:
+            suffix(2 * g)
+            suffix(2 * g + 1)
     pltpu.make_async_copy(qbuf.at[pl.ds(1, 15)], qbuf.at[pl.ds(1, 15)], q_sem).wait()
-    unit(x, 0, x, 1)
+    unit(x, 0, x, 1, first=True)
     unit(x, 2, x, 3)
 
     def middle(i, carry):
@@ -183,42 +215,62 @@
         return carry
 
     lax.fori_loop(0, 12, middle, 0)
+    def finish(plane):
+        r = pl.ds(128 * plane, 128)
+        whole = jnp.sum(tot[:, r], axis=0, keepdims=True)
+        lsrc[plane] = top[:, r] * SCALE + jnp.log(whole)
+        osrc[pl.ds(2 * plane, 2)] = (acc[:, r] / whole).T.astype(BF16).reshape(2, 64, HD)
+
+    def give(plane):
+        for cc in range(2):
+
+            def send():
+                for src, dst, sem in (
+                    (lsrc.at[plane], lbuf.at[2 * z + cc], l_sem),
+                    (osrc.at[2 * plane + cc], obuf.at[2 * z + cc], o_sem),
+                ):
+                    pltpu.make_async_remote_copy(
+                        src_ref=src, dst_ref=dst, send_sem=sem.at[0], recv_sem=sem.at[1],
+                        device_id=device(x, y, plane, other(cc)), device_id_type=MESH,
+                    ).start()
+
+            if cc:
+                send()
+            else:
+                pl.when(z != plane)(send)
+
+    ready = []
+
+    def after(j):
+        held = list(ready)
+        ready.clear()
+        for plane in (2 * j, 2 * j + 1):
+            finish(plane)
+            ready.append(plane)
+        for plane in held:
+            give(plane)
+
     far = wrap(x + 4)
     for g in range(2):
         hop(12 + g, far, g, True).wait_recv()
         hop(12 + g, far, g + 2, False).wait_recv()
-        unit(far, g, far, g + 2)
-
-    eye = lax.broadcasted_iota(jnp.int32, (64, HD), 0) == lax.broadcasted_iota(
-        jnp.int32, (64, HD), 1
-    )
-
-    def finish(s):
-        r = pl.ds(64 * s, 64)
-        whole = jnp.sum(tot[r, :], axis=1, keepdims=True)
-        osrc[s] = (acc[r, :] / whole).astype(BF16)
-        lse = top[r, :] * SCALE + jnp.log(whole)
-        lsrc[s] = jnp.sum(jnp.where(eye, lse, 0.0), axis=0, keepdims=True)
-
-    def give(d, cc):
-        pc, s = other(cc), 2 * d + cc
-        dev = device(x, y, wrap(z + d), pc)
-        slot = ((-d) % RING) * 2 + cc
-        remote(lsrc.at[s], lbuf.at[slot], l_sem, dev)
-        remote(osrc.at[s], obuf.at[slot], o_sem, dev)
-
-    order = list(reversed(zpeers))
-    finish(2 * order[0][0] + order[0][1])
-    for here, after in zip(order, order[1:] + [(0, 0)]):
-        finish(2 * after[0] + after[1])
-        give(*here)
-    obuf[0] = osrc[0]
-    lbuf[0] = lsrc[0]
-
-    pltpu.make_async_copy(lbuf.at[pl.ds(1, 15)], lbuf.at[pl.ds(1, 15)], l_sem).wait()
-    pltpu.make_async_copy(obuf.at[pl.ds(1, 15)], obuf.at[pl.ds(1, 15)], o_sem).wait()
+        unit(far, g, far, g + 2, after=after if g else None)
+    obuf[2 * z] = osrc[2 * z]
+    lbuf[2 * z] = lsrc[z]
+    for plane in ready:
+        give(plane)
+
+    def all_of(ref, sem):
+        rest = ref.at[pl.ds(0, 15)]
+        return pltpu.make_async_copy(rest, rest, sem)
+
+    all_of(lbuf, l_sem.at[1]).wait()
+    all_of(obuf, o_sem.at[1]).wait()
     for kk in range(2):
         k = other(kk)
+        eye = lax.broadcasted_iota(jnp.int32, (64, HD), 0) + 64 * kk == lax.broadcasted_iota(
+            jnp.int32, (64, HD), 1
+        )
         sx = smax[k].reshape(64, HD)
         lses = []
         for d in range(RING):
@@ -240,6 +292,8 @@
 
     for copy in sends:
         copy.wait_send()
+    all_of(lbuf, l_sem.at[0]).wait()
+    all_of(obuf, o_sem.at[0]).wait()
 
     def drain(i, carry):
         hop(i, x, 0, True).wait_send()
@@ -251,36 +305,40 @@
 
 def local(prefix_kv, queries, suffix_cache, suffix_lengths):
     vmem = pl.BlockSpec(memory_space=pltpu.VMEM)
+    hbm = pl.BlockSpec(memory_space=pltpu.HBM)
     dma = pltpu.SemaphoreType.DMA
     return pl.pallas_call(
         kernel,
         out_shape=jax.ShapeDtypeStruct(queries.shape, BF16),
         in_specs=[
-            vmem, vmem, pl.BlockSpec(memory_space=pltpu.SMEM), pl.BlockSpec(memory_space=pl.ANY),
+            hbm, hbm, hbm, hbm,
         ],
         out_specs=vmem,
         scratch_shapes=[
+            pltpu.VMEM((256, HD), BF16),
+            pltpu.VMEM((2, 4, 16, HD), BF16),
+            pltpu.SMEM((4,), jnp.int32),
             pltpu.VMEM((8, 16, 2, 32, HD), BF16),
             pltpu.VMEM((256, HD), F32),
             pltpu.VMEM((4, 2, 32, HD), BF16),
             pltpu.VMEM((2, 64, HD), BF16),
             pltpu.VMEM((16, 64, HD), BF16),
             pltpu.VMEM((4, 2048, HD), BF16),
-            pltpu.VMEM((1024, HD), F32),
-            pltpu.VMEM((1024, HD), F32),
-            pltpu.VMEM((1024, HD), F32),
+            pltpu.VMEM((1, 1024), F32),
+            pltpu.VMEM((8, 1024), F32),
+            pltpu.VMEM((HD, 1024), F32),
             pltpu.VMEM((16, 64, HD), BF16),
-            pltpu.VMEM((16, 1, HD), F32),
+            pltpu.VMEM((8, 1, HD), F32),
             pltpu.VMEM((16, 64, HD), BF16),
             pltpu.VMEM((16, 1, HD), F32),
             pltpu.VMEM((2, 8, 8, HD), F32),
             pltpu.VMEM((2, 8, 8, HD), F32),
             pltpu.VMEM((2, 8, 8, HD), F32),
             pltpu.VMEM((2, 8, 8, HD), F32),
-            dma, dma((60,)), dma((4,)), dma, dma((2, 14)), dma((2, 14)), dma, dma,
+            dma((4,)), dma((30,)), dma((4,)), dma, dma((2, 14)), dma((2, 14)), dma((2,)), dma((2,)),
         ],
         compiler_params=pltpu.CompilerParams(
-            collective_id=0, has_side_effects=True, vmem_limit_bytes=48 * 1024 * 1024
+            collective_id=0, has_side_effects=True, vmem_limit_bytes=66961408
         ),
     )(
         prefix_kv.reshape(256, HD), queries, suffix_lengths,

time: 73.5 us -> 60.7 us (0.83)
  Pallas kernels: 68.3 us -> 58.8 us
  local copies, waits for them, and re-layouts: 4.46 us -> 1.38 us
    pallas_call x1, Pallas kernels: 68.3 us -> 58.8 us  [local(): pl.pallas_call(kernel, out_shape=jax.ShapeDtypeStruct(queries.shape, BF16...]
    unnamed x9 -> x1, local copies, waits for them, and re-layouts: 4.46 us -> 1.38 us
where the time goes in v2:
time: 60.7 us; the launch traced here: 60.2 us
  Pallas kernels  58.8 us (97%)
  local copies, waits for them, and re-layouts  1.38 us (2%)
    pallas_call x1, Pallas kernels, local(): pl.pallas_call(kernel, out_shape=jax.ShapeDtypeStruct(queries.shape, BF16...  58.8 us
    unnamed x1, local copies, waits for them, and re-layouts  1.38 us

profile of v2, /device:TPU:1, one launch (start us, length us, event | category | flops | bytes accessed | tf_op | source)
XLA Modules:
  0.0 60.2 jit_solution(16023646151486862238)
XLA Ops:
  0.0 58.8 %shard_map.46 = bf16[2,4,16,128]{3,2,1,0:T(8,128)(2,1)} custom-call(bf16[256,128]{1,0:T(8,128)(2,1)} %bitcast.3, bf16[2,4,16,128]{3,2,1,0:T(8,128)(2,1)} %q_hbm.1, s32[4]{0:T(128)} %len_hbm.1, bf16[4,2048,128]{2,1,0:T(8,128)(2,1)} %bitcast.2), custom_call_target="tpu_custom_call" | custom-call | tf_op jit(solution)/shard_map/pallas_call | solution.py:310
  58.8 1.4 %copy.6 = bf16[2,4,16,128]{3,2,1,0:T(8,128)(2,1)} copy(bf16[2,4,16,128]{3,2,1,0:T(8,128)(2,1)} %shard_map.46) | data formatting | bytes 65536

commit v3 on v2

--- a/solution.py
+++ b/solution.py
@@ -24,9 +24,9 @@
 
 def kernel(
     pre_hbm, q_hbm, len_hbm, suf_hbm, out_ref,
-    pre_ref, q_ref, len_ref, kvbuf, kvf, kvsrc, qsrc, qbuf, sufbuf, top, tot, acc, osrc, lsrc, obuf, lbuf,
+    pre_ref, q_ref, len_ref, kvbuf, kvs, xbuf, kvf, kvsrc, qsrc, qbuf, sufbuf, top, tot, acc, osrc, lsrc, obuf, lbuf,
     sacc, smax, ssum, ob,
-    in_sem, send_sem, y_sem, q_sem, xr_sem, xl_sem, o_sem, l_sem,
+    in_sem, send_sem, ys_sem, f_sem, sd_sem, s_sem, y_sem, q_sem, xr_sem, xl_sem, o_sem, l_sem,
 ):
     x = lax.axis_index("rep")
     c = lax.axis_index("ctx")
@@ -66,7 +66,6 @@
     for r in range(8):
         kvsrc[r // 2, r % 2] = kvf[pl.ds(r, 32, stride=8), :].astype(BF16)
     my_head = 2 * hd + core
-    kvbuf[x, 0] = kvsrc[my_head]
     q8 = q_ref[...].reshape(8, 16, HD).astype(F32)
     for k in range(2):
         qsrc[k] = q8[:, 8 * k : 8 * k + 8, :].reshape(64, HD).astype(BF16)
@@ -85,22 +84,66 @@
         sends.append(copy)
 
     slot_of = {d: i for i, d in enumerate(ORDER)}
-    for i, d, cc in ypeers:
-        yy, pc = wrap(y + d), other(cc)
-        slot = slot_of[(-d) % RING] * 2 + cc
-        remote(
-            kvsrc.at[2 * lax.rem(yy, 2) + pc], kvbuf.at[x, slot],
-            y_sem.at[slot // 4], device(x, yy, z, pc),
+    right, left = device(wrap(x + 1), y, z, core), device(wrap(x - 1), y, z, core)
+
+    for cr, (src_rows, dst_rows) in enumerate(((32, 0), (16, 32))):
+
+        @pl.when(core == cr)
+        def _():
+            for d in ORDER:
+                for pc in (cr, 1 - cr):
+                    yy = wrap(y + d)
+                    src = kvsrc.at[2 * lax.rem(yy, 2) + pc, :, pl.ds(0, src_rows)]
+                    slot = slot_of[(-d) % RING]
+                    dst = kvbuf.at[x, slot, :, pl.ds(dst_rows, src_rows)]
+                    sem = y_sem.at[slot // 2]
+                    if (d, pc) == (0, cr):
+                        pltpu.make_async_copy(src, dst, sem).start()
+                    else:
+                        pltpu.make_async_remote_copy(
+                            src_ref=src, dst_ref=dst, send_sem=ys_sem, recv_sem=sem,
+                            device_id=device(x, yy, z, pc), device_id_type=MESH,
+                        ).start()
+
+    late_rows = pl.ds(16, 16)
+
+    def first(i, block, to_right):
+        way = 0 if to_right else 1
+        ref = xbuf.at[pl.ds(4 * block, 4)]
+        return pltpu.make_async_remote_copy(
+            src_ref=kvsrc.at[:, :, late_rows] if i == 0 else ref, dst_ref=ref,
+            send_sem=f_sem.at[way, 0, i], recv_sem=f_sem.at[way, 1, i],
+            device_id=right if to_right else left, device_id_type=MESH,
         )
+
+    def spread(block, own=False):
+        for d in ORDER:
+            yy = wrap(y + d)
+            slot = slot_of[(-d) % RING]
+            for pc in (1, 0):
+                head = 2 * lax.rem(yy, 2) + pc
+                src = kvsrc.at[head, :, late_rows] if own else xbuf.at[4 * block + head]
+                dst, sem = kvs.at[block, slot], s_sem.at[block]
+                if (d, pc) == (0, 1):
+                    pltpu.make_async_copy(src, dst, sem).start()
+                else:
+                    pltpu.make_async_remote_copy(
+                        src_ref=src, dst_ref=dst, send_sem=sd_sem, recv_sem=sem,
+                        device_id=device(x, yy, z, pc), device_id_type=MESH,
+                    ).start()
+
+    @pl.when(core == 1)
+    def _():
+        first(0, x, True).start()
+        first(0, x, False).start()
+
     for d, cc in zpeers:
         pc = other(cc)
         remote(qsrc.at[pc], qbuf.at[2 * z + cc], q_sem, device(x, y, wrap(z + d), pc))
 
-    right, left = device(wrap(x + 1), y, z, core), device(wrap(x - 1), y, z, core)
-
     def hop(i, slot, g, to_right):
         sem = xr_sem if to_right else xl_sem
-        ref = kvbuf.at[slot, pl.ds(4 * g, 4)]
+        ref = kvbuf.at[slot, pl.ds(2 * g, 2)]
         return pltpu.make_async_remote_copy(
             src_ref=ref, dst_ref=ref, send_sem=sem.at[0, i], recv_sem=sem.at[1, i],
             device_id=right if to_right else left, device_id_type=MESH,
@@ -133,10 +176,27 @@
 
     def unit(sa, ga, sb, gb, first=False, after=None):
         def part(slot, g, which):
-            return kvbuf[slot, pl.ds(4 * g, 4), which].reshape(128, HD)
+            return kvbuf[slot, pl.ds(2 * g, 2), which].reshape(96, HD)
 
         k = jnp.concatenate([part(sa, ga, 0), part(sb, gb, 0)], axis=0)
-        v = jnp.concatenate([part(sa, ga, 1), part(sb, gb, 1)], axis=0).T
+        v = jnp.concatenate([part(sa, ga, 1), part(sb, gb, 1)], axis=0)
+        attend(k, v, first, after)
+
+    def late_unit(sa, sb):
+        for slot in (sa, sb):
+            pltpu.make_async_copy(kvs.at[slot], kvs.at[slot], s_sem.at[slot]).wait()
+
+        def part(slot, which):
+            return kvs[slot, :, which].reshape(128, HD)
+
+        k = jnp.concatenate([part(sa, 0), part(sb, 0)], axis=0)
+        v = jnp.concatenate([part(sa, 1), part(sb, 1)], axis=0)
+        attend(k, v)
+
+    def attend(k, v, first=False, after=None):
+        rows = k.shape[0]
+        v = v.T
+
         def scores(j):
             q = qbuf[4 * j : 4 * j + 4].reshape(256, HD)
             return lax.dot_general(k, q, (((1,), (1,)), ((), ())), preferred_element_type=F32)
@@ -150,7 +210,7 @@
                 new = jnp.maximum(old, new)
                 keep = jnp.exp2((old - new) * (SCALE * LOG2E))
             p = jnp.exp2((s - new) * (SCALE * LOG2E))
-            part_sum = jnp.sum(p.reshape(32, 8, 256), axis=0)
+            part_sum = jnp.sum(p.reshape(rows // 8, 8, 256), axis=0)
             if not first:
                 part_sum = tot[:, r] * keep + part_sum
             top[:, r] = new
@@ -176,11 +236,23 @@
         gather(*late)
 
     for g in range(4):
-        lo = 1 if g == 0 else 4 * g
-        piece = kvbuf.at[x, pl.ds(lo, 4 * g + 4 - lo)]
+        piece = kvbuf.at[x, pl.ds(2 * g, 2)]
         pltpu.make_async_copy(piece, piece, y_sem.at[g]).wait()
         hop(g, x, g, True).start()
         hop(g, x, g, False).start()
+
+        @pl.when(core == 1)
+        def _():
+            if g == 0:
+                spread(x, own=True)
+            for to_right in (True, False):
+                if g < 3 or to_right:
+                    block = wrap(x - g - 1) if to_right else wrap(x + g + 1)
+                    first(g, block, to_right).wait_recv()
+                    if g < (3 if to_right else 2):
+                        first(g + 1, block, to_right).start()
+                    spread(block)
+
         if g == 0:
             fetch[2].wait()
             fetch[3].wait()
@@ -214,7 +286,11 @@
         unit(sl, g, sr, g)
         return carry
 
-    lax.fori_loop(0, 12, middle, 0)
+    lax.fori_loop(0, 8, middle, 0)
+    late_unit(x, wrap(x - 1))
+    lax.fori_loop(8, 12, middle, 0)
+    late_unit(wrap(x + 1), wrap(x - 2))
+    late_unit(wrap(x + 2), wrap(x - 3))
     def finish(plane):
         r = pl.ds(128 * plane, 128)
         whole = jnp.sum(tot[:, r], axis=0, keepdims=True)
@@ -255,6 +331,8 @@
         hop(12 + g, far, g, True).wait_recv()
         hop(12 + g, far, g + 2, False).wait_recv()
         unit(far, g, far, g + 2, after=after if g else None)
+        if g == 0:
+            late_unit(wrap(x + 3), far)
     obuf[2 * z] = osrc[2 * z]
     lbuf[2 * z] = lsrc[z]
     for plane in ready:
@@ -292,6 +370,21 @@
 
     for copy in sends:
         copy.wait_send()
+
+    @pl.when(core == 0)
+    def _():
+        all_of(qbuf, ys_sem).wait()
+
+    @pl.when(core == 1)
+    def _():
+        all_of(xbuf, ys_sem).wait()
+        block = kvbuf.at[pl.ds(0, 5)]
+        pltpu.make_async_copy(block, block, sd_sem).wait()
+        for i in range(4):
+            first(i, x, True).wait_send()
+            if i < 3:
+                first(i, x, False).wait_send()
+
     all_of(lbuf, l_sem.at[0]).wait()
     all_of(obuf, o_sem.at[0]).wait()
 
@@ -309,7 +402,7 @@
     dma = pltpu.SemaphoreType.DMA
     return pl.pallas_call(
         kernel,
-        out_shape=jax.ShapeDtypeStruct(queries.shape, BF16),
+        out_shape=pltpu.VMEM(queries.shape, BF16),
         in_specs=[
             hbm, hbm, hbm, hbm,
         ],
@@ -318,7 +411,9 @@
             pltpu.VMEM((256, HD), BF16),
             pltpu.VMEM((2, 4, 16, HD), BF16),
             pltpu.SMEM((4,), jnp.int32),
-            pltpu.VMEM((8, 16, 2, 32, HD), BF16),
+            pltpu.VMEM((8, 8, 2, 48, HD), BF16),
+            pltpu.VMEM((8, 8, 2, 16, HD), BF16),
+            pltpu.VMEM((32, 2, 16, HD), BF16),
             pltpu.VMEM((256, HD), F32),
             pltpu.VMEM((4, 2, 32, HD), BF16),
             pltpu.VMEM((2, 64, HD), BF16),
@@ -335,14 +430,19 @@
             pltpu.VMEM((2, 8, 8, HD), F32),
             pltpu.VMEM((2, 8, 8, HD), F32),
             pltpu.VMEM((2, 8, 8, HD), F32),
-            dma((4,)), dma((30,)), dma((4,)), dma, dma((2, 14)), dma((2, 14)), dma((2,)), dma((2,)),
+            dma((4,)), dma((15,)), dma, dma((2, 2, 4)), dma, dma((8,)), dma((4,)), dma, dma((2, 14)), dma((2, 14)), dma((2,)), dma((2,)),
         ],
         compiler_params=pltpu.CompilerParams(
             collective_id=0, has_side_effects=True, vmem_limit_bytes=66961408
         ),
     )(
-        prefix_kv.reshape(256, HD), queries, suffix_lengths,
-        suffix_cache.reshape(4, 2048, HD),
+        *(
+            pltpu.with_memory_space_constraint(a, pltpu.HBM)
+            for a in (
+                prefix_kv.reshape(256, HD), queries, suffix_lengths,
+                suffix_cache.reshape(4, 2048, HD),
+            )
+        ),
     )
 
 

time: 60.7 us -> 56.9 us (0.937)
  Pallas kernels: 58.8 us -> 56.2 us
  local copies, waits for them, and re-layouts: 1.38 us -> 0.62 us
    pallas_call x1, Pallas kernels: 58.8 us -> 56.2 us  [local(): pl.pallas_call(kernel, out_shape=pltpu.VMEM(queries.shape, BF16), in_spec...]
    unnamed x1, local copies, waits for them, and re-layouts: 1.38 us -> 0.62 us
where the time goes in v3:
time: 56.9 us; the launch traced here: 56.8 us
  Pallas kernels  56.2 us (99%)
  local copies, waits for them, and re-layouts  0.62 us (1%)
    pallas_call x1, Pallas kernels, local(): pl.pallas_call(kernel, out_shape=pltpu.VMEM(queries.shape, BF16), in_spec...  56.2 us

profile of v3, /device:TPU:1, one launch (start us, length us, event | category | flops | bytes accessed | tf_op | source)
XLA Modules:
  0.0 56.8 jit_solution(1957073469308905119)
XLA Ops:
  0.0 56.2 %shard_map.46 = bf16[2,4,16,128]{3,2,1,0:T(8,128)(2,1)S(1)} custom-call(bf16[256,128]{1,0:T(8,128)(2,1)} %bitcast.3, bf16[2,4,16,128]{3,2,1,0:T(8,128)(2,1)} %q_hbm.1, s32[4]{0:T(128)} %len_hbm.1, bf16[4,2048,128]{2,1,0:T(8,128)(2,1)} %bitcast.2), custom_call_target="tpu_custom_call" | custom-call | tf_op jit(solution)/shard_map/pallas_call | solution.py:403
  56.2 0.6 %copy.6 = bf16[2,4,16,128]{3,2,1,0:T(8,128)(2,1)} copy(bf16[2,4,16,128]{3,2,1,0:T(8,128)(2,1)S(1)} %shard_map.46) | data formatting | bytes 65536

commit v4 on v3

--- a/solution.py
+++ b/solution.py
@@ -57,7 +57,7 @@
     greet = [device(x, wrap(y + d), z, other(cc)) for _, d, cc in ypeers]
     greet += [device(x, y, wrap(z + d), other(cc)) for d, cc in zpeers if d]
     greet += [device(wrap(x + 1), y, z, core), device(wrap(x - 1), y, z, core)]
-    for dev in greet:
+    for dev in greet[14::-1] + greet[:14:-1]:
         pl.semaphore_signal(barrier, inc=1, device_id=dev, device_id_type=MESH)
 
     fetch[0].wait()
@@ -318,13 +318,11 @@
     ready = []
 
     def after(j):
-        held = list(ready)
-        ready.clear()
         for plane in (2 * j, 2 * j + 1):
             finish(plane)
+            if ready:
+                give(ready.pop())
             ready.append(plane)
-        for plane in held:
-            give(plane)
 
     far = wrap(x + 4)
     for g in range(2):
@@ -343,28 +341,31 @@
         return pltpu.make_async_copy(rest, rest, sem)
 
     all_of(lbuf, l_sem.at[1]).wait()
-    all_of(obuf, o_sem.at[1]).wait()
+    shares = []
     for kk in range(2):
         k = other(kk)
         eye = lax.broadcasted_iota(jnp.int32, (64, HD), 0) + 64 * kk == lax.broadcasted_iota(
             jnp.int32, (64, HD), 1
         )
         sx = smax[k].reshape(64, HD)
-        lses = []
-        for d in range(RING):
-            spread = jnp.where(eye, lbuf[2 * d + kk], 0.0)
-            lses.append(jnp.sum(spread, axis=1, keepdims=True))
+        lses = [
+            jnp.sum(jnp.where(eye, lbuf[2 * d + kk], 0.0), axis=1, keepdims=True)
+            for d in range(RING)
+        ]
         best = sx
         for v in lses:
             best = jnp.maximum(best, v)
-        w = jnp.exp2((sx - best) * LOG2E)
-        num = w * sacc[k].reshape(64, HD)
-        den = w * ssum[k].reshape(64, HD)
-        for d in range(RING):
-            w = jnp.exp2((lses[d] - best) * LOG2E)
+        own = jnp.exp2((sx - best) * LOG2E)
+        ws = [jnp.exp2((v - best) * LOG2E) for v in lses]
+        den = own * ssum[k].reshape(64, HD)
+        for w in ws:
+            den = den + w
+        shares.append((own * sacc[k].reshape(64, HD), ws, den))
+    all_of(obuf, o_sem.at[1]).wait()
+    for kk, (num, ws, den) in enumerate(shares):
+        for d, w in enumerate(ws):
             num = num + w * obuf[2 * d + kk].astype(F32)
-            den = den + w
-        ob[k] = (num / den).reshape(8, 8, HD)
+        ob[other(kk)] = (num / den).reshape(8, 8, HD)
     both = jnp.stack([ob[0], ob[1]], axis=1).reshape(8, 16, HD)
     out_ref[...] = both.astype(BF16).reshape(2, 4, 16, HD)
 

time: 56.9 us -> 56.3 us (0.989)
  Pallas kernels: 56.2 us -> 55.5 us
    pallas_call x1, Pallas kernels: 56.2 us -> 55.5 us  [local(): pl.pallas_call(kernel, out_shape=pltpu.VMEM(queries.shape, BF16), in_spec...]
where the time goes in v4:
time: 56.3 us; the launch traced here: 56.1 us
  Pallas kernels  55.5 us (99%)
  local copies, waits for them, and re-layouts  0.62 us (1%)
    pallas_call x1, Pallas kernels, local(): pl.pallas_call(kernel, out_shape=pltpu.VMEM(queries.shape, BF16), in_spec...  55.5 us

profile of v4, /device:TPU:1, one launch (start us, length us, event | category | flops | bytes accessed | tf_op | source)
XLA Modules:
  0.0 56.1 jit_solution(744710347306636752)
XLA Ops:
  0.0 55.5 %shard_map.46 = bf16[2,4,16,128]{3,2,1,0:T(8,128)(2,1)S(1)} custom-call(bf16[256,128]{1,0:T(8,128)(2,1)} %bitcast.3, bf16[2,4,16,128]{3,2,1,0:T(8,128)(2,1)} %q_hbm.1, s32[4]{0:T(128)} %len_hbm.1, bf16[4,2048,128]{2,1,0:T(8,128)(2,1)} %bitcast.2), custom_call_target="tpu_custom_call" | custom-call | tf_op jit(solution)/shard_map/pallas_call | solution.py:404
  55.5 0.6 %copy.6 = bf16[2,4,16,128]{3,2,1,0:T(8,128)(2,1)} copy(bf16[2,4,16,128]{3,2,1,0:T(8,128)(2,1)S(1)} %shard_map.46) | data formatting | bytes 65536

commit v5 on v4

--- a/solution.py
+++ b/solution.py
@@ -256,9 +256,6 @@
         if g == 0:
             fetch[2].wait()
             fetch[3].wait()
-        if g < 2:
-            suffix(2 * g)
-            suffix(2 * g + 1)
     pltpu.make_async_copy(qbuf.at[pl.ds(1, 15)], qbuf.at[pl.ds(1, 15)], q_sem).wait()
     unit(x, 0, x, 1, first=True)
     unit(x, 2, x, 3)
@@ -286,7 +283,9 @@
         unit(sl, g, sr, g)
         return carry
 
-    lax.fori_loop(0, 8, middle, 0)
+    for n in range(4):
+        lax.fori_loop(2 * n, 2 * n + 2, middle, 0)
+        suffix(n)
     late_unit(x, wrap(x - 1))
     lax.fori_loop(8, 12, middle, 0)
     late_unit(wrap(x + 1), wrap(x - 2))

time: 56.3 us -> 58.1 us (1.032)
  Pallas kernels: 55.5 us -> 57.3 us
    pallas_call x1, Pallas kernels: 55.5 us -> 57.3 us  [local(): pl.pallas_call(kernel, out_shape=pltpu.VMEM(queries.shape, BF16), in_spec...]
where the time goes in v5:
time: 58.1 us; the launch traced here: 57.9 us
  Pallas kernels  57.3 us (99%)
  local copies, waits for them, and re-layouts  0.62 us (1%)
    pallas_call x1, Pallas kernels, local(): pl.pallas_call(kernel, out_shape=pltpu.VMEM(queries.shape, BF16), in_spec...  57.3 us

profile of v5, /device:TPU:1, one launch (start us, length us, event | category | flops | bytes accessed | tf_op | source)
XLA Modules:
  0.0 57.9 jit_solution(16558991387059284537)
XLA Ops:
  0.0 57.3 %shard_map.46 = bf16[2,4,16,128]{3,2,1,0:T(8,128)(2,1)S(1)} custom-call(bf16[256,128]{1,0:T(8,128)(2,1)} %bitcast.3, bf16[2,4,16,128]{3,2,1,0:T(8,128)(2,1)} %q_hbm.1, s32[4]{0:T(128)} %len_hbm.1, bf16[4,2048,128]{2,1,0:T(8,128)(2,1)} %bitcast.2), custom_call_target="tpu_custom_call" | custom-call | tf_op jit(solution)/shard_map/pallas_call | solution.py:403
  57.3 0.6 %copy.6 = bf16[2,4,16,128]{3,2,1,0:T(8,128)(2,1)} copy(bf16[2,4,16,128]{3,2,1,0:T(8,128)(2,1)S(1)} %shard_map.46) | data formatting | bytes 65536
